TPU v7x, 256 devices: a whole 4x4x8 slice. The times are simulated.
256 devices in a mesh: dp: 16 (over z_hi, y), fsdp: 16 (over x, z_lo, core).
Axes of the slice: x: 4, y: 4, z: 8 (z_hi: 4, z_lo: 2; z = z_hi * 2 + z_lo), core: 2. Of those that a mesh axis runs over, the one named last changes fastest.
Arguments:
- features: bfloat16 [49152, 8192], P(('dp', 'fsdp')), may hold values from -6 to 6
- grad_out: bfloat16 [49152, 8192], P(('dp', 'fsdp')), may hold values from -6 to 6
- weight_tiles: bfloat16 [256, 128, 128], P('fsdp'), may hold values from -0.25 to 0.25
- tile_row: int32 [256], replicated, may hold values from 0 to 63, as said below
- tile_column: int32 [256], replicated, may hold values from 0 to 63, as said below
Outputs:
- grad_features: bfloat16 [49152, 8192], P(('dp', 'fsdp'))
- tile_update: float32 [256, 128, 128], P('fsdp')
Inputs may be any that keep to these rules, and one draw needn't show every extreme that they name: `tile_row`: every tile-row holds exactly 4 stored tiles; the tile-columns of tile-row i are i XOR s for the four values s in (0, 2^a, 2^b, 2^a + 2^b), with two distinct bits a, b drawn per run; the stored order is a random permutation of the pattern. Every tile-column holds exactly 4 stored tiles; no (tile_row, tile_column) pair appears twice.
All inputs are finite; a program needn't handle non-finite values.
Results may differ from a plain program's by a relative error of at most 0.0034.
Values may be sent and summed in bfloat16 or wider, within the bound.
No kernel may reach another device: no remote copies, remote signals or barrier semaphores. Data moves between devices by JAX's collectives and lax.ppermute only.
A program may use at most 128 MiB of HBM per device.

v0:
```python
import math
import jax
import jax.numpy as jnp
from jax import lax
from jax.sharding import PartitionSpec as P


def gelu_slope(value):
    root_term = math.sqrt(2.0 / math.pi)
    inner = root_term * (value + 0.044715 * value * value * value)
    hyper = jnp.tanh(inner)
    return 0.5 * (1.0 + hyper) + 0.5 * value * (1.0 - hyper * hyper) * root_term * (
        1.0 + 3.0 * 0.044715 * value * value
    )


def on_device(features, grad_out, weight_tiles, tile_row, tile_column):
    rows_here = features.shape[0]
    side = weight_tiles.shape[1]
    nblocks = features.shape[1] // side
    total_tiles = tile_row.shape[0]
    per_block = total_tiles // nblocks
    feature_blocks = features.reshape(rows_here, nblocks, side)
    grad_blocks = grad_out.reshape(rows_here, nblocks, side)
    order_rows = jnp.argsort(tile_row, stable=True)
    order_columns = jnp.argsort(tile_column, stable=True)
    columns_by_row = tile_column[order_rows].reshape(nblocks, per_block)
    rows_by_column = tile_row[order_columns].reshape(nblocks, per_block)
    whole = lax.all_gather(weight_tiles, "fsdp", axis=0, tiled=True)
    tiles_by_row = whole[order_rows].reshape(nblocks, per_block, side, side)
    taken = feature_blocks[:, columns_by_row]
    preact = jnp.einsum("rnkc,nkcd->rnd", taken, tiles_by_row, preferred_element_type=jnp.float32)
    slope_grad = (grad_blocks.astype(jnp.float32) * gelu_slope(preact)).astype(jnp.bfloat16)
    tiles_by_column = whole[order_columns].reshape(nblocks, per_block, side, side)
    slopes_taken = slope_grad[:, rows_by_column]
    returned = jnp.einsum(
        "rnkd,nkcd->rnc", slopes_taken, tiles_by_column, preferred_element_type=jnp.float32
    )
    grad_features = (
        (grad_blocks.astype(jnp.float32) + returned)
        .astype(jnp.bfloat16)
        .reshape(rows_here, nblocks * side)
    )
    tile_ids = jnp.arange(
        total_tiles // lax.axis_size("fsdp") * lax.axis_size("fsdp"), dtype=jnp.int32
    )
    columns = tile_column[tile_ids]
    row_ids = tile_row[tile_ids]
    picked = jnp.take(feature_blocks, columns, axis=1)
    slopes = jnp.take(slope_grad, row_ids, axis=1)
    summed = lax.psum_scatter(
        jnp.einsum("rnc,rnd->ncd", picked, slopes, preferred_element_type=jnp.float32),
        "fsdp",
        scatter_dimension=0,
        tiled=True,
    )
    weight_grad = lax.psum(summed, "dp")
    tile_update = weight_grad * lax.rsqrt(
        jnp.mean(weight_grad * weight_grad, axis=(1, 2), keepdims=True) + 1e-06
    )
    return (grad_features, tile_update)


def solution(mesh):
    return jax.shard_map(
        on_device,
        mesh=mesh,
        in_specs=(
            P(("dp", "fsdp"), None),
            P(("dp", "fsdp"), None),
            P("fsdp", None, None),
            P(),
            P(),
        ),
        out_specs=(P(("dp", "fsdp"), None), P("fsdp", None, None)),
        check_vma=False,
    )
```

profile of v0, /device:TPU:8, one launch (start us, length us, event | category | flops | bytes accessed | tf_op | source)
XLA Modules:
  0.0 482.4 jit_solution(4299826176216152528)
XLA Ops:
  7.2 0.0 copy-start
  7.2 0.0 all-gather.2.cloned.1.call-start
  7.2 0.7 all-gather.2.cloned.1.call-update
  7.9 0.0 reduce-scatter.2.cloned.1.call-start
  8.0 4.0 sort.32
  12.0 2.0 gather_fusion.7
  13.9 2.0 gather_fusion.6
  16.0 2.0 gather_fusion.2
  17.9 0.1 reshape.97
  18.1 0.1 reshape.143
  18.2 0.0 copy-done
  18.2 2.6 copy_bitcast_fusion.1
  20.7 0.0 copy-start.4
  20.7 12.8 %gather_fusion.3 = bf16[256,192,128]{2,1,0:T(8,128)(2,1)} fusion(bf16[192,64,128]{2,0,1:T(8,128)(2,1)} %copy_bitcast_fusion.1, s32[1024]{0:T(1024)S(1)} %pad_clamp_fusion.4), kind=kCustom, calls=%fused_computation.5 | custom fusion | bytes 25166848 | tf_op jit(solution)/shard_map/gather | solution.py:31
  33.6 0.0 copy-done.4
  33.6 10.8 %gather_fusion.8 = bf16[256,192,128]{2,1,0:T(8,128)(2,1)} fusion(bf16[192,64,128]{2,0,1:T(8,128)(2,1)S(1)} %copy-done.4, s32[1024]{0:T(1024)S(1)} %pad_clamp_fusion.1), kind=kCustom, calls=%fused_computation.clone | custom fusion | bytes 25166848 | tf_op jit(solution)/shard_map/jit(_take)/gather | solution.py:49
  44.4 23.1 %all-gather.2.cloned.1.call-done = bf16[256,128,128]{2,1,0:T(8,128)(2,1)} async-done(((bf16[16,128,128]{2,1,0:T(8,128)(2,1)}), bf16[256,128,128]{2,1,0:T(8,128)(2,1)}) %all-gather.2.cloned.1.call-update) | async-done | bytes 8388624 | tf_op jit(solution)/shard_map/all_gather | solution.py:29
  67.5 12.1 %gather_fusion.1 = bf16[256,128,128]{2,1,0:T(8,128)(2,1)} fusion(bf16[256,128,128]{2,1,0:T(8,128)(2,1)} %all-gather.2.cloned.1.call-done, s32[1024]{0:T(1024)S(1)} %pad_clamp_fusion.5), kind=kCustom, calls=%fused_computation.3 | custom fusion | bytes 16778240 | tf_op jit(solution)/shard_map/gather | solution.py:30
  79.6 11.0 %fusion.13 = bf16[192,64,128]{2,0,1:T(8,128)(2,1)S(1)} fusion(bf16[192,64,4,128]{3,0,2,1:T(8,128)(2,1)} %bitcast.65, bf16[64,4,128,128]{3,2,1,0:T(8,128)(2,1)} %bitcast.68, bf16[192,8192]{1,0:T(8,128)(2,1)} %param.8), kind=kOutput, calls=%fused_computation.25 | convolution fusion | flops 1642070016 | bytes 27262976 | tf_op jit(solution)/shard_map/rnkc,nkcd->rnd/dot_general | solution.py:32
  90.6 0.0 copy-start.5
  90.6 10.7 %gather_fusion.9 = bf16[256,192,128]{2,1,0:T(8,128)(2,1)} fusion(bf16[192,64,128]{2,0,1:T(8,128)(2,1)S(1)} %fusion.13, s32[1024]{0:T(1024)S(1)} %pad_clamp_fusion), kind=kCustom, calls=%fused_computation.1.clone | custom fusion | bytes 25166848 | tf_op jit(solution)/shard_map/jit(_take)/gather | solution.py:50
  101.4 0.0 copy-done.5
  101.4 14.6 %fusion = f32[256,128,128]{2,1,0:T(8,128)} fusion(bf16[256,192,128]{2,1,0:T(8,128)(2,1)} %gather_fusion.9, bf16[256,192,128]{2,1,0:T(8,128)(2,1)} %gather_fusion.8, pred[256]{0:T(512)(128)(4,1)S(1)} %get-tuple-element.7, pred[256]{0:T(512)(128)(4,1)S(1)} %get-tuple-element.8), kind=kOutput, calls=%fused_computation.10 | convolution fusion | flops 1623195648 | bytes 41943552 | tf_op jit(solution)/shard_map/rnc,rnd->ncd/dot_general | solution.py:52
  116.0 0.0 copy-start.2
  116.0 0.0 copy-start.3
  116.0 0.0 reduce-scatter.2.cloned.1.call-update
  116.0 0.0 all-reduce.2.cloned.1.call-start
  116.1 0.6 copy-done.2
  116.7 3.2 sort.31
  119.9 0.0 copy-done.3
  119.9 2.2 gather_fusion.4
  122.1 0.1 reshape.98
  122.2 0.1 reshape.159
  122.3 12.4 %gather_fusion.5 = bf16[256,192,128]{2,1,0:T(8,128)(2,1)} fusion(bf16[192,64,128]{2,0,1:T(8,128)(2,1)} %copy-done.5, s32[1024]{0:T(1024)S(1)} %pad_clamp_fusion.3), kind=kCustom, calls=%fused_computation.7 | custom fusion | bytes 25166848 | tf_op jit(solution)/shard_map/gather | solution.py:35
  134.7 12.2 %gather_fusion = bf16[256,128,128]{2,1,0:T(8,128)(2,1)} fusion(bf16[256,128,128]{2,1,0:T(8,128)(2,1)} %all-gather.2.cloned.1.call-done, s32[1024]{0:T(1024)S(1)} %pad_clamp_fusion.6), kind=kCustom, calls=%fused_computation.2 | custom fusion | bytes 16778240 | tf_op jit(solution)/shard_map/gather | solution.py:34
  146.9 155.1 %reduce-scatter.2.cloned.1.call-done = f32[16,128,128]{2,1,0:T(8,128)} async-done(((f32[256,128,128]{2,1,0:T(8,128)}), f32[16,128,128]{2,1,0:T(8,128)}) %reduce-scatter.2.cloned.1.call-update) | async-done | bytes 1048592 | tf_op jit(solution)/shard_map/reduce_scatter | solution.py:51
  301.9 0.0 all-reduce.2.cloned.1.call-update
  302.0 0.0 copy-start.1
  302.0 12.5 %fusion.18 = bf16[64,24,8,128]{3,2,1,0:T(8,128)(2,1)} fusion(bf16[64,4,128,128]{3,2,1,0:T(8,128)(2,1)} %bitcast.67, bf16[192,64,4,128]{3,0,2,1:T(8,128)(2,1)} %bitcast.66, bf16[192,8192]{1,0:T(8,128)(2,1)} %param.8), kind=kOutput, calls=%fused_computation.33 | convolution fusion | flops 1615331328 | bytes 27262976 | tf_op jit(solution)/shard_map/rnkd,nkcd->rnc/dot_general | solution.py:36
  314.5 4.4 copy.32
  319.0 153.1 %all-reduce.2.cloned.1.call-done = f32[16,128,128]{2,1,0:T(8,128)} async-done(((f32[16,128,128]{2,1,0:T(8,128)}), f32[16,128,128]{2,1,0:T(8,128)}) %all-reduce.2.cloned.1.call-update) | async-done | bytes 1048592 | tf_op jit(solution)/shard_map/psum | solution.py:57
  472.1 1.4 multiply_reduce_fusion
  473.5 2.3 broadcast_multiply_fusion
  475.9 0.0 copy-done.1
  (18 shorter events, 0.1 us)
Async XLA Ops:
  7.2 11.0 %copy-start = (bf16[192,8192]{1,0:T(8,128)(2,1)S(1)}, bf16[192,8192]{1,0:T(8,128)(2,1)}, u32[]{:S(2)}) copy-start(bf16[192,8192]{1,0:T(8,128)(2,1)} %param.7) | copy-start | bytes 9437188
  7.2 60.3 %all-gather.2.cloned.1.call-start = ((), (), s32[]{:S(2)}) async-start(), calls=%async_computation.1 | async-start | bytes 8912896 | tf_op jit(solution)/shard_map/all_gather | solution.py:29
  7.9 294.0 %reduce-scatter.2.cloned.1.call-start = ((), (), s32[]{:S(2)}) async-start(), calls=%async_computation.2 | async-start | bytes 17825792 | tf_op jit(solution)/shard_map/reduce_scatter | solution.py:51
  20.7 12.9 %copy-start.4 = (bf16[192,64,128]{2,0,1:T(8,128)(2,1)S(1)}, bf16[192,64,128]{2,0,1:T(8,128)(2,1)}, u32[]{:S(2)}) copy-start(bf16[192,64,128]{2,0,1:T(8,128)(2,1)} %copy_bitcast_fusion.1) | copy-start | bytes 9437188
  90.6 10.7 %copy-start.5 = (bf16[192,64,128]{2,0,1:T(8,128)(2,1)}, bf16[192,64,128]{2,0,1:T(8,128)(2,1)S(1)}, u32[]{:S(2)}) copy-start(bf16[192,64,128]{2,0,1:T(8,128)(2,1)S(1)} %fusion.13) | copy-start | bytes 9437188
  116.0 0.7 copy-start.2
  116.0 3.9 copy-start.3
  116.0 356.1 %all-reduce.2.cloned.1.call-start = ((), (), s32[]{:S(2)}) async-start(), calls=%async_computation.3 | async-start | bytes 2097152 | tf_op jit(solution)/shard_map/psum | solution.py:57
  302.0 173.9 %copy-start.1 = (bf16[192,8192]{1,0:T(8,128)(2,1)S(1)}, bf16[192,8192]{1,0:T(8,128)(2,1)}, u32[]{:S(2)}) copy-start(bf16[192,8192]{1,0:T(8,128)(2,1)} %param.7) | copy-start | bytes 9437188
Sparse Core Ops, SparseCore 0:
  9.9 57.6 all-gather.1
  116.2 185.7 reduce-scatter.1
  304.6 167.4 all-reduce.1
where the time goes:
time: 483 us; the launch traced here: 482 us
  waiting for transfers between devices  332 us (69%)
  local copies, waits for them, and re-layouts  87.2 us (18%)
  matrix products  38.2 us (8%)
  between operations  13.9 us (3%)
  other arithmetic  11 us (2%)
    reduce_scatter x1, waiting for transfers between devices, on_device(): lax.psum_scatter(jnp.einsum('rnc,rnd->ncd', picked, slopes, preferred_ele...  155 us
    psum x1, waiting for transfers between devices, on_device(): weight_grad = lax.psum(summed, 'dp')  153 us
    all_gather x1, waiting for transfers between devices, on_device(): whole = lax.all_gather(weight_tiles, 'fsdp', axis=0, tiled=True)  23.1 us
    dot_general x1, matrix products, on_device(): jnp.einsum('rnc,rnd->ncd', picked, slopes, preferred_element_type=jnp.flo...  14.6 us
    gather x1, local copies, waits for them, and re-layouts, on_device(): taken = feature_blocks[:, columns_by_row]  12.8 us
    dot_general x1, matrix products, on_device(): jnp.einsum('rnkd,nkcd->rnc', slopes_taken, tiles_by_column, preferred_ele...  12.5 us
    gather x1, local copies, waits for them, and re-layouts, on_device(): slopes_taken = slope_grad[:, rows_by_column]  12.4 us
    gather x1, local copies, waits for them, and re-layouts, on_device(): whole[order_columns].reshape(nblocks, per_block, side, side)  12.2 us
  transfers between devices with their start and end apart: 3, of which 3 were waited for; matrix products, arithmetic and copies ran while one was open for 17% of the time, Pallas kernels for 0%

commit v1 on v0

--- a/solution.py
+++ b/solution.py
@@ -54,7 +54,7 @@
         scatter_dimension=0,
         tiled=True,
     )
-    weight_grad = lax.psum(summed, "dp")
+    weight_grad = jnp.sum(lax.all_gather(summed, "dp"), axis=0)
     tile_update = weight_grad * lax.rsqrt(
         jnp.mean(weight_grad * weight_grad, axis=(1, 2), keepdims=True) + 1e-06
     )

time: 483 us -> 525 us (1.087)
  the two profiles are of different devices: /device:TPU:8 before, /device:TPU:2 now
where the time goes in v1:
time: 525 us; the launch traced here: 524 us
  waiting for transfers between devices  369 us (70%)
  local copies, waits for them, and re-layouts  85.1 us (16%)
  matrix products  36.9 us (7%)
  other arithmetic  19.6 us (4%)
  between operations  13.9 us (3%)
    reduce_scatter x1, waiting for transfers between devices, on_device(): lax.psum_scatter(jnp.einsum('rnc,rnd->ncd', picked, slopes, preferred_ele...  184 us
    all_gather x1, waiting for transfers between devices, on_device(): weight_grad = jnp.sum(lax.all_gather(summed, 'dp'), axis=0)  161 us
    all_gather x1, waiting for transfers between devices, on_device(): whole = lax.all_gather(weight_tiles, 'fsdp', axis=0, tiled=True)  23 us
    dot_general x1, matrix products, on_device(): jnp.einsum('rnc,rnd->ncd', picked, slopes, preferred_element_type=jnp.flo...  14.6 us
    gather x1, local copies, waits for them, and re-layouts, on_device(): slopes_taken = slope_grad[:, rows_by_column]  12.9 us
    gather x1, local copies, waits for them, and re-layouts, on_device(): taken = feature_blocks[:, columns_by_row]  12.8 us
    gather x1, local copies, waits for them, and re-layouts, on_device(): whole[order_columns].reshape(nblocks, per_block, side, side)  12.1 us
    gather x1, local copies, waits for them, and re-layouts, on_device(): tiles_by_row = whole[order_rows].reshape(nblocks, per_block, side, side)  12.1 us
  transfers between devices with their start and end apart: 3, of which 3 were waited for; matrix products, arithmetic and copies ran while one was open for 15% of the time, Pallas kernels for 0%

profile of v1, /device:TPU:2, one launch (start us, length us, event | category | flops | bytes accessed | tf_op | source)
XLA Modules:
  0.0 524.4 jit_solution(17040093149918109024)
XLA Ops:
  7.2 0.0 copy-start
  7.2 0.0 all-gather.4.cloned.1.call-start
  7.2 0.7 all-gather.4.cloned.1.call-update
  7.9 0.0 reduce-scatter.2.cloned.1.call-start
  8.0 4.0 sort.32
  12.0 2.0 gather_fusion.7
  13.9 2.0 gather_fusion.6
  16.0 2.0 gather_fusion.2
  17.9 0.1 reshape.97
  18.1 0.1 reshape.143
  18.2 0.0 copy-done
  18.2 2.6 copy_bitcast_fusion.1
  20.7 0.0 copy-start.4
  20.7 12.8 %gather_fusion.3 = bf16[256,192,128]{2,1,0:T(8,128)(2,1)} fusion(bf16[192,64,128]{2,0,1:T(8,128)(2,1)} %copy_bitcast_fusion.1, s32[1024]{0:T(1024)S(1)} %pad_clamp_fusion.4), kind=kCustom, calls=%fused_computation.5 | custom fusion | bytes 25166848 | tf_op jit(solution)/shard_map/gather | solution.py:31
  33.6 0.0 copy-done.4
  33.6 10.8 %gather_fusion.8 = bf16[256,192,128]{2,1,0:T(8,128)(2,1)} fusion(bf16[192,64,128]{2,0,1:T(8,128)(2,1)S(1)} %copy-done.4, s32[1024]{0:T(1024)S(1)} %pad_clamp_fusion.1), kind=kCustom, calls=%fused_computation.clone | custom fusion | bytes 25166848 | tf_op jit(solution)/shard_map/jit(_take)/gather | solution.py:49
  44.4 23.0 %all-gather.4.cloned.1.call-done = bf16[256,128,128]{2,1,0:T(8,128)(2,1)} async-done(((bf16[16,128,128]{2,1,0:T(8,128)(2,1)}), bf16[256,128,128]{2,1,0:T(8,128)(2,1)}) %all-gather.4.cloned.1.call-update) | async-done | bytes 8388624 | tf_op jit(solution)/shard_map/all_gather | solution.py:29
  67.4 12.1 %gather_fusion.1 = bf16[256,128,128]{2,1,0:T(8,128)(2,1)} fusion(bf16[256,128,128]{2,1,0:T(8,128)(2,1)} %all-gather.4.cloned.1.call-done, s32[1024]{0:T(1024)S(1)} %pad_clamp_fusion.5), kind=kCustom, calls=%fused_computation.3 | custom fusion | bytes 16778240 | tf_op jit(solution)/shard_map/gather | solution.py:30
  79.5 11.0 %fusion.13 = bf16[192,64,128]{2,0,1:T(8,128)(2,1)S(1)} fusion(bf16[192,64,4,128]{3,0,2,1:T(8,128)(2,1)} %bitcast.67, bf16[64,4,128,128]{3,2,1,0:T(8,128)(2,1)} %bitcast.70, bf16[192,8192]{1,0:T(8,128)(2,1)} %param.8), kind=kOutput, calls=%fused_computation.25 | convolution fusion | flops 1642070016 | bytes 27262976 | tf_op jit(solution)/shard_map/rnkc,nkcd->rnd/dot_general | solution.py:32
  90.5 0.0 copy-start.5
  90.5 10.7 %gather_fusion.9 = bf16[256,192,128]{2,1,0:T(8,128)(2,1)} fusion(bf16[192,64,128]{2,0,1:T(8,128)(2,1)S(1)} %fusion.13, s32[1024]{0:T(1024)S(1)} %pad_clamp_fusion), kind=kCustom, calls=%fused_computation.1.clone | custom fusion | bytes 25166848 | tf_op jit(solution)/shard_map/jit(_take)/gather | solution.py:50
  101.3 0.0 copy-done.5
  101.3 14.6 %fusion = f32[256,128,128]{2,1,0:T(8,128)} fusion(bf16[256,192,128]{2,1,0:T(8,128)(2,1)} %gather_fusion.9, bf16[256,192,128]{2,1,0:T(8,128)(2,1)} %gather_fusion.8, pred[256]{0:T(512)(128)(4,1)S(1)} %get-tuple-element.7, pred[256]{0:T(512)(128)(4,1)S(1)} %get-tuple-element.8), kind=kOutput, calls=%fused_computation.10 | convolution fusion | flops 1623195648 | bytes 41943552 | tf_op jit(solution)/shard_map/rnc,rnd->ncd/dot_general | solution.py:52
  115.9 0.0 copy-start.2
  115.9 0.0 copy-start.3
  115.9 0.0 reduce-scatter.2.cloned.1.call-update
  115.9 0.0 all-gather.6.cloned.1.call-start
  116.0 183.9 %reduce-scatter.2.cloned.1.call-done = f32[16,128,128]{2,1,0:T(8,128)} async-done(((f32[256,128,128]{2,1,0:T(8,128)}), f32[16,128,128]{2,1,0:T(8,128)}) %reduce-scatter.2.cloned.1.call-update) | async-done | bytes 1048592 | tf_op jit(solution)/shard_map/reduce_scatter | solution.py:51
  299.9 0.0 all-gather.6.cloned.1.call-update
  299.9 0.0 copy-done.2
  299.9 3.2 sort.31
  303.1 0.0 copy-done.3
  303.1 2.2 gather_fusion.4
  305.3 0.1 reshape.98
  305.5 0.1 reshape.159
  305.6 12.9 %gather_fusion.5 = bf16[256,192,128]{2,1,0:T(8,128)(2,1)} fusion(bf16[192,64,128]{2,0,1:T(8,128)(2,1)} %copy-done.5, s32[1024]{0:T(1024)S(1)} %pad_clamp_fusion.3), kind=kCustom, calls=%fused_computation.7 | custom fusion | bytes 25166848 | tf_op jit(solution)/shard_map/gather | solution.py:35
  318.4 12.1 %gather_fusion = bf16[256,128,128]{2,1,0:T(8,128)(2,1)} fusion(bf16[256,128,128]{2,1,0:T(8,128)(2,1)} %all-gather.4.cloned.1.call-done, s32[1024]{0:T(1024)S(1)} %pad_clamp_fusion.6), kind=kCustom, calls=%fused_computation.2 | custom fusion | bytes 16778240 | tf_op jit(solution)/shard_map/gather | solution.py:34
  330.6 11.2 %fusion.18 = bf16[64,24,8,128]{3,2,1,0:T(8,128)(2,1)S(1)} fusion(bf16[64,4,128,128]{3,2,1,0:T(8,128)(2,1)} %bitcast.69, bf16[192,64,4,128]{3,0,2,1:T(8,128)(2,1)} %bitcast.68, bf16[192,8192]{1,0:T(8,128)(2,1)} %param.8), kind=kOutput, calls=%fused_computation.33 | convolution fusion | flops 1615331328 | bytes 27262976 | tf_op jit(solution)/shard_map/rnkd,nkcd->rnc/dot_general | solution.py:36
  341.8 2.5 copy.32
  344.3 161.1 %all-gather.6.cloned.1.call-done = f32[256,128,128]{2,1,0:T(8,128)} async-done(((f32[16,128,128]{2,1,0:T(8,128)}), f32[256,128,128]{2,1,0:T(8,128)}) %all-gather.6.cloned.1.call-update) | async-done | bytes 16777232 | tf_op jit(solution)/shard_map/all_gather | solution.py:57
  505.5 0.0 copy-start.1
  505.5 8.6 %reduce_sum.18 = f32[16,128,128]{2,1,0:T(8,128)} reduce(f32[16,16,128,128]{3,2,1,0:T(8,128)} %bitcast.66, f32[]{:T(128)} %constant.10.clone.1), dimensions={0}, to_apply=%region_3.5 | reduce | flops 3932160 | bytes 17825796 | tf_op jit(solution)/shard_map/reduce_sum | solution.py:57
  514.0 1.4 multiply_reduce_fusion
  515.5 2.3 broadcast_multiply_fusion
  517.8 0.0 copy-done.1
  (18 shorter events, 0.1 us)
Async XLA Ops:
  7.2 11.0 %copy-start = (bf16[192,8192]{1,0:T(8,128)(2,1)S(1)}, bf16[192,8192]{1,0:T(8,128)(2,1)}, u32[]{:S(2)}) copy-start(bf16[192,8192]{1,0:T(8,128)(2,1)} %param.7) | copy-start | bytes 9437188
  7.2 60.2 %all-gather.4.cloned.1.call-start = ((), (), s32[]{:S(2)}) async-start(), calls=%async_computation.1 | async-start | bytes 8912896 | tf_op jit(solution)/shard_map/all_gather | solution.py:29
  7.9 292.0 %reduce-scatter.2.cloned.1.call-start = ((), (), s32[]{:S(2)}) async-start(), calls=%async_computation.2 | async-start | bytes 17825792 | tf_op jit(solution)/shard_map/reduce_scatter | solution.py:51
  20.7 12.9 %copy-start.4 = (bf16[192,64,128]{2,0,1:T(8,128)(2,1)S(1)}, bf16[192,64,128]{2,0,1:T(8,128)(2,1)}, u32[]{:S(2)}) copy-start(bf16[192,64,128]{2,0,1:T(8,128)(2,1)} %copy_bitcast_fusion.1) | copy-start | bytes 9437188
  90.5 10.7 %copy-start.5 = (bf16[192,64,128]{2,0,1:T(8,128)(2,1)}, bf16[192,64,128]{2,0,1:T(8,128)(2,1)S(1)}, u32[]{:S(2)}) copy-start(bf16[192,64,128]{2,0,1:T(8,128)(2,1)S(1)} %fusion.13) | copy-start | bytes 9437188
  115.9 184.0 %copy-start.2 = (s32[256]{0:T(256)S(1)}, s32[256]{0:T(256)}, u32[]{:S(2)}) copy-start(s32[256]{0:T(256)} %param.11) | copy-start | bytes 3076
  115.9 187.2 %copy-start.3 = (s32[256]{0:T(256)S(1)}, s32[256]{0:T(256)}, u32[]{:S(2)}) copy-start(s32[256]{0:T(256)} %param.10) | copy-start | bytes 3076
  115.9 389.5 %all-gather.6.cloned.1.call-start = ((), (), s32[]{:S(2)}) async-start(), calls=%async_computation.3 | async-start | bytes 17825792 | tf_op jit(solution)/shard_map/all_gather | solution.py:57
  505.5 12.4 %copy-start.1 = (bf16[192,8192]{1,0:T(8,128)(2,1)S(1)}, bf16[192,8192]{1,0:T(8,128)(2,1)}, u32[]{:S(2)}) copy-start(bf16[192,8192]{1,0:T(8,128)(2,1)} %param.7) | copy-start | bytes 9437188
Sparse Core Ops, SparseCore 0:
  9.9 57.5 all-gather.3
  116.1 183.7 reduce-scatter.1
  302.3 203.1 all-gather.5
